TPU v7x, 256 devices: a whole 4x4x8 slice. The times are simulated.
256 devices in a mesh: seq: 32 (over y, x, core), head: 8 (over z).
Axes of the slice: x: 4, y: 4, z: 8, core: 2. Of those that a mesh axis runs over, the one named last changes fastest.
Arguments:
- queries: bfloat16 [32768, 8192], P(('seq', 'head')), may hold values from -6 to 6
- key_vectors: bfloat16 [32768, 8192], P(('seq', 'head')), may hold values from -6 to 6
- value_vectors: bfloat16 [32768, 8192], P(('seq', 'head')), may hold values from -6 to 6
- out_gain: float32 [64, 128], P('head'), may hold values from 0.1 to 1.9
Outputs:
- attended: bfloat16 [32768, 8192], P(('seq', 'head'))
All inputs are finite; a program needn't handle non-finite values.
Results may differ from a plain program's by a relative error of at most 0.0049.
Values may be sent and summed in bfloat16 or wider, within the bound.
A program may use at most 128 MiB of HBM per device.

v0:
```python
import jax
import jax.numpy as jnp
from jax import lax
from jax.sharding import PartitionSpec as P

HEADS = 64
HD = 128


def shifted(block, axis, distance):
    count = lax.axis_size(axis)
    return lax.ppermute(block, axis, [(i, i + distance) for i in range(count - distance)])


def seq_exclusive(own):
    count = lax.axis_size("seq")
    total = own
    distance = 1
    while distance < count:
        total = total + shifted(total, "seq", distance)
        distance *= 2
    return shifted(total, "seq", 1)


def per_device(queries, key_vectors, value_vectors, out_gain):
    tokens = queries.shape[0]
    query_heads = queries.reshape(tokens, HEADS, HD)
    key_heads = key_vectors.reshape(tokens, HEADS, HD)
    value_heads = value_vectors.reshape(tokens, HEADS, HD)
    states = jnp.einsum("bhd,bhe->hde", key_heads, value_heads, preferred_element_type=jnp.float32)
    gathered = lax.all_to_all(
        states.astype(jnp.bfloat16).reshape(8, HEADS // 8, HD, HD),
        "head",
        split_axis=0,
        concat_axis=0,
        tiled=True,
    ).astype(jnp.float32)
    gain = lax.all_gather(out_gain, "head", axis=0, tiled=True)
    prefix = seq_exclusive(jnp.sum(gathered, axis=0))
    running = prefix
    parts = []
    for z in range(8):
        parts.append(running.astype(jnp.bfloat16))
        running = running + gathered[z]
    carried = lax.all_to_all(jnp.stack(parts), "head", split_axis=0, concat_axis=0, tiled=True)
    carried = carried.reshape(HEADS, HD, HD)
    inter = jnp.einsum("bhd,hde->bhe", query_heads, carried, preferred_element_type=jnp.float32)
    scores = jnp.einsum("bhd,chd->hbc", query_heads, key_heads, preferred_element_type=jnp.float32)
    causal = jnp.arange(tokens)[:, None] >= jnp.arange(tokens)[None, :]
    scores = jnp.where(causal[None], scores, jnp.float32(0.0)).astype(jnp.bfloat16)
    intra = jnp.einsum("hbc,chd->bhd", scores, value_heads, preferred_element_type=jnp.float32)
    raw = inter + intra
    scale = lax.rsqrt(jnp.mean(raw * raw, axis=-1, keepdims=True) + 1e-06)
    normed = (raw * scale * gain[None]).astype(jnp.bfloat16)
    return normed.reshape(tokens, HEADS * HD)


def solution(mesh):
    return jax.shard_map(
        per_device,
        mesh=mesh,
        in_specs=(
            P(("seq", "head"), None),
            P(("seq", "head"), None),
            P(("seq", "head"), None),
            P("head", None),
        ),
        out_specs=P(("seq", "head"), None),
        check_vma=False,
    )
```

profile of v0, /device:TPU:56, one launch (start us, length us, event | category | flops | bytes accessed | tf_op | source)
XLA Modules:
  0.0 247.2 jit_solution(813136822619654408)
XLA Ops:
  0.0 4.2 %copy.11 = bf16[128,8192]{0,1:T(8,128)(2,1)} copy(bf16[128,8192]{1,0:T(8,128)(2,1)} %param.5) | data formatting | bytes 4194304 | tf_op jit(solution)/shard_map/reshape | solution.py:28
  4.2 4.1 %copy.12 = bf16[128,8192]{0,1:T(8,128)(2,1)} copy(bf16[128,8192]{1,0:T(8,128)(2,1)} %param.6) | data formatting | bytes 4194304 | tf_op jit(solution)/shard_map/reshape | solution.py:29
  8.3 3.8 %convolution_convert_fusion = bf16[64,128,128]{2,1,0:T(8,128)(2,1)S(1)} fusion(bf16[128,64,128]{0,2,1:T(8,128)(2,1)} %bitcast.108, bf16[128,64,128]{0,2,1:T(8,128)(2,1)} %bitcast.110), kind=kOutput, calls=%fused_computation.7 | convolution fusion | flops 269484032 | bytes 6291456 | tf_op jit(solution)/shard_map/bhd,bhe->hde/dot_general | solution.py:30
  12.1 58.1 %all_to_all.10 = bf16[8,8,128,128]{3,2,1,0:T(8,128)(2,1)S(1)} all-to-all(bf16[8,8,128,128]{3,2,1,0:T(8,128)(2,1)S(1)} %bitcast.113), channel_id=1, replica_groups=mesh['seq'=32,'head'=8] {'head'}, dimensions={0} | all-to-all | bytes 4194304 | tf_op jit(solution)/shard_map/all_to_all | solution.py:31
  70.2 0.4 convert_reduce_fusion
  70.5 1.9 collective-permute-start
  72.5 10.7 %collective-permute-done = f32[8,128,128]{2,1,0:T(8,128)S(1)} collective-permute-done((f32[8,128,128]{2,1,0:T(8,128)S(1)}, f32[8,128,128]{2,1,0:T(8,128)S(1)}, u32[]{:S(2)}, u32[]{:S(2)}) %collective-permute-start) | collective-permute-done | bytes 524320 | tf_op jit(solution)/shard_map/ppermute | solution.py:12
  83.2 1.9 collective-permute-start.1
  85.1 12.9 %collective-permute-done.1 = f32[8,128,128]{2,1,0:T(8,128)S(1)} collective-permute-done((f32[8,128,128]{2,1,0:T(8,128)S(1)}, f32[8,128,128]{2,1,0:T(8,128)S(1)}, u32[]{:S(2)}, u32[]{:S(2)}) %collective-permute-start.1) | collective-permute-done | bytes 524320 | tf_op jit(solution)/shard_map/ppermute | solution.py:12
  98.1 2.5 %collective-permute-start.2 = (f32[8,128,128]{2,1,0:T(8,128)S(1)}, f32[8,128,128]{2,1,0:T(8,128)S(1)}, u32[]{:S(2)}, u32[]{:S(2)}) collective-permute-start(f32[8,128,128]{2,1,0:T(8,128)S(1)} %add.51), channel_id=1, source_target_pairs={{0,32},{8,40},{16,48},{24,56},{32,64},{40,72},{48,80},{56,88},{64,... | collective-permute-start | bytes 1572872 | tf_op jit(solution)/shard_map/ppermute | solution.py:12
  100.7 11.8 %collective-permute-done.2 = f32[8,128,128]{2,1,0:T(8,128)S(1)} collective-permute-done((f32[8,128,128]{2,1,0:T(8,128)S(1)}, f32[8,128,128]{2,1,0:T(8,128)S(1)}, u32[]{:S(2)}, u32[]{:S(2)}) %collective-permute-start.2) | collective-permute-done | bytes 524320 | tf_op jit(solution)/shard_map/ppermute | solution.py:12
  112.5 1.3 collective-permute-start.3
  113.8 9.9 %collective-permute-done.3 = f32[8,128,128]{2,1,0:T(8,128)S(1)} collective-permute-done((f32[8,128,128]{2,1,0:T(8,128)S(1)}, f32[8,128,128]{2,1,0:T(8,128)S(1)}, u32[]{:S(2)}, u32[]{:S(2)}) %collective-permute-start.3) | collective-permute-done | bytes 524320 | tf_op jit(solution)/shard_map/ppermute | solution.py:12
  123.7 1.3 collective-permute-start.4
  125.0 11.3 %collective-permute-done.4 = f32[8,128,128]{2,1,0:T(8,128)S(1)} collective-permute-done((f32[8,128,128]{2,1,0:T(8,128)S(1)}, f32[8,128,128]{2,1,0:T(8,128)S(1)}, u32[]{:S(2)}, u32[]{:S(2)}) %collective-permute-start.4) | collective-permute-done | bytes 524320 | tf_op jit(solution)/shard_map/ppermute | solution.py:12
  136.3 1.9 collective-permute-start.5
  138.3 0.5 convert_element_type.37
  138.8 10.2 %collective-permute-done.5 = f32[8,128,128]{2,1,0:T(8,128)S(1)} collective-permute-done((f32[8,128,128]{2,1,0:T(8,128)S(1)}, f32[8,128,128]{2,1,0:T(8,128)S(1)}, u32[]{:S(2)}, u32[]{:S(2)}) %collective-permute-start.5) | collective-permute-done | bytes 524320 | tf_op jit(solution)/shard_map/ppermute | solution.py:12
  149.0 0.7 bitcast_dynamic-update-slice_fusion.6
  149.7 0.8 bitcast_dynamic-update-slice_fusion.5
  150.4 0.8 bitcast_dynamic-update-slice_fusion.4
  151.2 0.8 bitcast_dynamic-update-slice_fusion.3
  152.0 0.8 bitcast_dynamic-update-slice_fusion.2
  152.8 0.8 bitcast_dynamic-update-slice_fusion.1
  153.6 0.8 bitcast_dynamic-update-slice_fusion
  154.4 0.8 fusion.16
  155.2 5.8 %all-to-all-start.1 = ((bf16[8,8,128,128]{3,2,1,0:T(8,128)(2,1)}), bf16[8,8,128,128]{3,2,1,0:T(8,128)(2,1)}, u32[]{:S(2)}, u32[]{:S(2)}) async-start(bf16[8,8,128,128]{3,2,1,0:T(8,128)(2,1)} %fusion.16), calls=%async_computation.1 | async-start | bytes 4194304 | tf_op jit(solution)/shard_map/all_to_all | solution.py:45
  161.0 65.5 %all_gather.3 = f32[64,128]{1,0:T(8,128)S(1)} all-gather(f32[8,128]{1,0:T(8,128)S(1)} %copy-done.1), channel_id=1, replica_groups=mesh['seq'=32,'head'=8] {'head'}, dimensions={0}, use_global_device_ids=true | all-gather | bytes 36864 | tf_op jit(solution)/shard_map/all_gather | solution.py:38
  226.5 5.1 %fusion.1 = f32[64,128,128]{2,1,0:T(8,128)} fusion(bf16[64,128,128]{2,1,0:T(8,128)(2,1)} %bitcast.21, bf16[128,8192]{1,0:T(8,128)(2,1)S(1)} %copy-done), kind=kOutput, calls=%fused_computation.5 | convolution fusion | flops 268435456 | bytes 8388608 | tf_op jit(solution)/shard_map/bhd,hde->bhe/dot_general | solution.py:47
  231.7 7.6 %multiply_reduce_fusion = (f32[128,64]{0,1:T(8,128)S(1)}, f32[128,64,128]{0,2,1:T(8,128)}) fusion(bf16[128,64,128]{0,2,1:T(8,128)(2,1)} %bitcast.111, bf16[128,64,128]{0,2,1:T(8,128)(2,1)} %bitcast.109, pred[128,128]{1,0:T(8,128)(4,1)S(1)} %iota_compare_fusion, f32[64,128,128]{2,1,0:T(8,128)} %fusion.1, bf16[128,8192]{1,0:T(8,128)(2,1)S(1)} %copy-done), kind=kOutput, calls=%fused_computation.2 | convolution fusion | flops 542105600 | bytes 14729216 | tf_op jit(solution)/shard_map/hbc,chd->bhd/dot_general | solution.py:51
  239.2 3.9 %multiply_convert_fusion = bf16[128,64,128]{0,2,1:T(8,128)(2,1)} fusion(f32[128,64,128]{0,2,1:T(8,128)} %get-tuple-element.10, f32[64,128]{1,0:T(8,128)S(1)} %all_gather.3, f32[128,64]{0,1:T(8,128)S(1)} %add_rsqrt_fusion), kind=kLoop, calls=%fused_computation.1 | loop fusion | flops 3145728 | bytes 6356992 | tf_op jit(solution)/shard_map/convert_element_type | solution.py:54
  243.1 4.1 %copy.10 = bf16[128,8192]{1,0:T(8,128)(2,1)} copy(bf16[128,8192]{0,1:T(8,128)(2,1)} %bitcast.112) | data formatting | bytes 4194304 | tf_op jit(solution)/shard_map/reshape | solution.py:55
  (12 shorter events, 0.3 us)
Async XLA Ops:
  0.0 226.5 %copy-start = (bf16[128,8192]{1,0:T(8,128)(2,1)S(1)}, bf16[128,8192]{1,0:T(8,128)(2,1)}, u32[]{:S(2)}) copy-start(bf16[128,8192]{1,0:T(8,128)(2,1)} %param.4) | copy-start | bytes 6291460
  70.5 12.6 %collective-permute-start = (f32[8,128,128]{2,1,0:T(8,128)S(1)}, f32[8,128,128]{2,1,0:T(8,128)S(1)}, u32[]{:S(2)}, u32[]{:S(2)}) collective-permute-start(f32[8,128,128]{2,1,0:T(8,128)S(1)} %convert_reduce_fusion), channel_id=1, source_target_pairs={{0,8},{8,16},{16,24},{24,32},{32,40},{40,48},{48,56},{56,64},{64,7... | collective-permute-start | bytes 1572872 | tf_op jit(solution)/shard_map/ppermute | solution.py:12
  83.2 14.8 %collective-permute-start.1 = (f32[8,128,128]{2,1,0:T(8,128)S(1)}, f32[8,128,128]{2,1,0:T(8,128)S(1)}, u32[]{:S(2)}, u32[]{:S(2)}) collective-permute-start(f32[8,128,128]{2,1,0:T(8,128)S(1)} %add.50), channel_id=1, source_target_pairs={{0,16},{8,24},{16,32},{24,40},{32,48},{40,56},{48,64},{56,72},{64,... | collective-permute-start | bytes 1572872 | tf_op jit(solution)/shard_map/ppermute | solution.py:12
  98.1 14.3 %collective-permute-start.2 = (f32[8,128,128]{2,1,0:T(8,128)S(1)}, f32[8,128,128]{2,1,0:T(8,128)S(1)}, u32[]{:S(2)}, u32[]{:S(2)}) collective-permute-start(f32[8,128,128]{2,1,0:T(8,128)S(1)} %add.51), channel_id=1, source_target_pairs={{0,32},{8,40},{16,48},{24,56},{32,64},{40,72},{48,80},{56,88},{64,... | collective-permute-start | bytes 1572872 | tf_op jit(solution)/shard_map/ppermute | solution.py:12
  112.5 11.2 %collective-permute-start.3 = (f32[8,128,128]{2,1,0:T(8,128)S(1)}, f32[8,128,128]{2,1,0:T(8,128)S(1)}, u32[]{:S(2)}, u32[]{:S(2)}) collective-permute-start(f32[8,128,128]{2,1,0:T(8,128)S(1)} %add.52), channel_id=1, source_target_pairs={{0,64},{8,72},{16,80},{24,88},{32,96},{40,104},{48,112},{56,120},{... | collective-permute-start | bytes 1572872 | tf_op jit(solution)/shard_map/ppermute | solution.py:12
  123.7 12.6 %collective-permute-start.4 = (f32[8,128,128]{2,1,0:T(8,128)S(1)}, f32[8,128,128]{2,1,0:T(8,128)S(1)}, u32[]{:S(2)}, u32[]{:S(2)}) collective-permute-start(f32[8,128,128]{2,1,0:T(8,128)S(1)} %add.53), channel_id=1, source_target_pairs={{0,128},{8,136},{16,144},{24,152},{32,160},{40,168},{48,176},{56,1... | collective-permute-start | bytes 1572872 | tf_op jit(solution)/shard_map/ppermute | solution.py:12
  136.3 12.6 %collective-permute-start.5 = (f32[8,128,128]{2,1,0:T(8,128)S(1)}, f32[8,128,128]{2,1,0:T(8,128)S(1)}, u32[]{:S(2)}, u32[]{:S(2)}) collective-permute-start(f32[8,128,128]{2,1,0:T(8,128)S(1)} %add.54), channel_id=1, source_target_pairs={{0,8},{8,16},{16,24},{24,32},{32,40},{40,48},{48,56},{56,64},{64,7... | collective-permute-start | bytes 1572872 | tf_op jit(solution)/shard_map/ppermute | solution.py:12
  155.2 5.8 %copy-start.1 = (f32[8,128]{1,0:T(8,128)S(1)}, f32[8,128]{1,0:T(8,128)}, u32[]{:S(2)}) copy-start(f32[8,128]{1,0:T(8,128)} %param.7) | copy-start | bytes 12292
  155.2 71.3 %all-to-all-start.1 = ((bf16[8,8,128,128]{3,2,1,0:T(8,128)(2,1)}), bf16[8,8,128,128]{3,2,1,0:T(8,128)(2,1)}, u32[]{:S(2)}, u32[]{:S(2)}) async-start(bf16[8,8,128,128]{3,2,1,0:T(8,128)(2,1)} %fusion.16), calls=%async_computation.1 | async-start | bytes 4194304 | tf_op jit(solution)/shard_map/all_to_all | solution.py:45
where the time goes:
time: 248 us; the launch traced here: 247 us
  blocking collectives  124 us (50%)
  waiting for transfers between devices  66.7 us (27%)
  starting transfers between devices  16.7 us (7%)
  matrix products  16.5 us (7%)
  local copies, waits for them, and re-layouts  12.3 us (5%)
  other arithmetic  11.3 us (5%)
    ppermute x6, waiting for transfers between devices, shifted(): lax.ppermute(block, axis, [(i, i + distance) for i in range(count - dista...  66.7 us
    all_gather x1, blocking collectives, per_device(): gain = lax.all_gather(out_gain, 'head', axis=0, tiled=True)  65.5 us
    all_to_all x1, blocking collectives, per_device(): lax.all_to_all(states.astype(jnp.bfloat16).reshape(8, HEADS // 8, HD, HD)...  58.1 us
    ppermute x6, starting transfers between devices, shifted(): lax.ppermute(block, axis, [(i, i + distance) for i in range(count - dista...  10.9 us
    dot_general x1, matrix products, per_device(): jnp.einsum('hbc,chd->bhd', scores, value_heads, preferred_element_type=jn...  7.56 us
    all_to_all x1, starting transfers between devices, per_device(): lax.all_to_all(jnp.stack(parts), 'head', split_axis=0, concat_axis=0, til...  5.8 us
    unnamed x7, other arithmetic  5.4 us
    dot_general x1, matrix products, per_device(): jnp.einsum('bhd,hde->bhe', query_heads, carried, preferred_element_type=j...  5.14 us
  transfers between devices with their start and end apart: 7, of which 6 were waited for; matrix products, arithmetic and copies ran while one was open for 0% of the time, Pallas kernels for 0%

commit v1 on v0

--- a/solution.py
+++ b/solution.py
@@ -35,7 +35,16 @@
         concat_axis=0,
         tiled=True,
     ).astype(jnp.float32)
-    gain = lax.all_gather(out_gain, "head", axis=0, tiled=True)
+    ways = lax.axis_size("head")
+    up = [(d, (d + 1) % ways) for d in range(ways)]
+    down = [(d, (d - 1) % ways) for d in range(ways)]
+    earlier, later = ([out_gain], [out_gain])
+    for _ in range(ways // 2):
+        earlier.append(lax.ppermute(earlier[-1], "head", up))
+    for _ in range((ways - 1) // 2):
+        later.append(lax.ppermute(later[-1], "head", down))
+    line = jnp.concatenate([*earlier[::-1], *later[1:]], axis=0)
+    gain = jnp.roll(line, (lax.axis_index("head") - ways // 2) * out_gain.shape[0], axis=0)
     prefix = seq_exclusive(jnp.sum(gathered, axis=0))
     running = prefix
     parts = []

time: 248 us -> 244 us (0.984); the launches traced: 247 us -> 240 us
  blocking collectives: 124 us -> 58.1 us
  waiting for transfers between devices: 66.7 us -> 113 us
  starting transfers between devices: 16.7 us -> 28.3 us
    all_gather x1 -> x0, blocking collectives: 65.5 us -> none  [per_device(): gain = lax.all_gather(out_gain, 'head', axis=0, tiled=True)]
    ppermute x0 -> x7, waiting for transfers between devices: none -> 46.7 us  [the longest x4 44.6 us: per_device(): earlier.append(lax.ppermute(earlier[-1], 'head', up))]
    ppermute x0 -> x7, starting transfers between devices: none -> 11.6 us  [the longest x4 8.3 us: per_device(): earlier.append(lax.ppermute(earlier[-1], 'head', up))]
  transfers between devices with their start and end apart: 7 -> 14, of which waited for: 6 -> 13; matrix products, arithmetic and copies ran while one was open for 0% -> 0% of each run, Pallas kernels for 0% -> 0%
where the time goes in v1:
time: 244 us; the launch traced here: 240 us
  waiting for transfers between devices  113 us (46%)
  blocking collectives  58.1 us (24%)
  starting transfers between devices  28.3 us (12%)
  matrix products  16.5 us (7%)
  local copies, waits for them, and re-layouts  12.4 us (5%)
  other arithmetic  11.4 us (5%)
    ppermute x6, waiting for transfers between devices, shifted(): lax.ppermute(block, axis, [(i, i + distance) for i in range(count - dista...  66.7 us
    all_to_all x1, blocking collectives, per_device(): lax.all_to_all(states.astype(jnp.bfloat16).reshape(8, HEADS // 8, HD, HD)...  58.1 us
    ppermute x4, waiting for transfers between devices, per_device(): earlier.append(lax.ppermute(earlier[-1], 'head', up))  44.6 us
    ppermute x6, starting transfers between devices, shifted(): lax.ppermute(block, axis, [(i, i + distance) for i in range(count - dista...  10.9 us
    ppermute x4, starting transfers between devices, per_device(): earlier.append(lax.ppermute(earlier[-1], 'head', up))  8.3 us
    dot_general x1, matrix products, per_device(): jnp.einsum('hbc,chd->bhd', scores, value_heads, preferred_element_type=jn...  7.57 us
    all_to_all x1, starting transfers between devices, per_device(): lax.all_to_all(jnp.stack(parts), 'head', split_axis=0, concat_axis=0, til...  5.81 us
    unnamed x7, other arithmetic  5.53 us
  transfers between devices with their start and end apart: 14, of which 13 were waited for; matrix products, arithmetic and copies ran while one was open for 0% of the time, Pallas kernels for 0%

profile of v1, /device:TPU:56, one launch (start us, length us, event | category | flops | bytes accessed | tf_op | source)
XLA Modules:
  0.0 240.3 jit_solution(6923871710528606555)
XLA Ops:
  0.0 4.2 %copy.11 = bf16[128,8192]{0,1:T(8,128)(2,1)} copy(bf16[128,8192]{1,0:T(8,128)(2,1)} %param.5) | data formatting | bytes 4194304 | tf_op jit(solution)/shard_map/reshape | solution.py:28
  4.2 4.1 %copy.12 = bf16[128,8192]{0,1:T(8,128)(2,1)} copy(bf16[128,8192]{1,0:T(8,128)(2,1)} %param.6) | data formatting | bytes 4194304 | tf_op jit(solution)/shard_map/reshape | solution.py:29
  8.3 3.8 %convolution_convert_fusion = bf16[64,128,128]{2,1,0:T(8,128)(2,1)S(1)} fusion(bf16[128,64,128]{0,2,1:T(8,128)(2,1)} %bitcast.108, bf16[128,64,128]{0,2,1:T(8,128)(2,1)} %bitcast.110), kind=kOutput, calls=%fused_computation.7 | convolution fusion | flops 269484032 | bytes 6291456 | tf_op jit(solution)/shard_map/bhd,bhe->hde/dot_general | solution.py:30
  12.1 58.1 %all_to_all.10 = bf16[8,8,128,128]{3,2,1,0:T(8,128)(2,1)S(1)} all-to-all(bf16[8,8,128,128]{3,2,1,0:T(8,128)(2,1)S(1)} %bitcast.113), channel_id=1, replica_groups=mesh['seq'=32,'head'=8] {'head'}, dimensions={0} | all-to-all | bytes 4194304 | tf_op jit(solution)/shard_map/all_to_all | solution.py:31
  70.5 1.9 collective-permute-start
  72.5 10.7 %collective-permute-done = f32[8,128,128]{2,1,0:T(8,128)S(1)} collective-permute-done((f32[8,128,128]{2,1,0:T(8,128)S(1)}, f32[8,128,128]{2,1,0:T(8,128)S(1)}, u32[]{:S(2)}, u32[]{:S(2)}) %collective-permute-start) | collective-permute-done | bytes 524320 | tf_op jit(solution)/shard_map/ppermute | solution.py:12
  83.2 1.9 collective-permute-start.1
  85.1 12.9 %collective-permute-done.1 = f32[8,128,128]{2,1,0:T(8,128)S(1)} collective-permute-done((f32[8,128,128]{2,1,0:T(8,128)S(1)}, f32[8,128,128]{2,1,0:T(8,128)S(1)}, u32[]{:S(2)}, u32[]{:S(2)}) %collective-permute-start.1) | collective-permute-done | bytes 524320 | tf_op jit(solution)/shard_map/ppermute | solution.py:12
  98.1 2.5 %collective-permute-start.2 = (f32[8,128,128]{2,1,0:T(8,128)S(1)}, f32[8,128,128]{2,1,0:T(8,128)S(1)}, u32[]{:S(2)}, u32[]{:S(2)}) collective-permute-start(f32[8,128,128]{2,1,0:T(8,128)S(1)} %add.62), channel_id=1, source_target_pairs={{0,32},{8,40},{16,48},{24,56},{32,64},{40,72},{48,80},{56,88},{64,... | collective-permute-start | bytes 1572872 | tf_op jit(solution)/shard_map/ppermute | solution.py:12
  100.7 11.8 %collective-permute-done.2 = f32[8,128,128]{2,1,0:T(8,128)S(1)} collective-permute-done((f32[8,128,128]{2,1,0:T(8,128)S(1)}, f32[8,128,128]{2,1,0:T(8,128)S(1)}, u32[]{:S(2)}, u32[]{:S(2)}) %collective-permute-start.2) | collective-permute-done | bytes 524320 | tf_op jit(solution)/shard_map/ppermute | solution.py:12
  112.5 1.3 collective-permute-start.3
  113.8 9.9 %collective-permute-done.3 = f32[8,128,128]{2,1,0:T(8,128)S(1)} collective-permute-done((f32[8,128,128]{2,1,0:T(8,128)S(1)}, f32[8,128,128]{2,1,0:T(8,128)S(1)}, u32[]{:S(2)}, u32[]{:S(2)}) %collective-permute-start.3) | collective-permute-done | bytes 524320 | tf_op jit(solution)/shard_map/ppermute | solution.py:12
  123.7 1.3 collective-permute-start.4
  125.0 11.3 %collective-permute-done.4 = f32[8,128,128]{2,1,0:T(8,128)S(1)} collective-permute-done((f32[8,128,128]{2,1,0:T(8,128)S(1)}, f32[8,128,128]{2,1,0:T(8,128)S(1)}, u32[]{:S(2)}, u32[]{:S(2)}) %collective-permute-start.4) | collective-permute-done | bytes 524320 | tf_op jit(solution)/shard_map/ppermute | solution.py:12
  136.4 1.9 collective-permute-start.5
  138.8 10.2 %collective-permute-done.5 = f32[8,128,128]{2,1,0:T(8,128)S(1)} collective-permute-done((f32[8,128,128]{2,1,0:T(8,128)S(1)}, f32[8,128,128]{2,1,0:T(8,128)S(1)}, u32[]{:S(2)}, u32[]{:S(2)}) %collective-permute-start.5) | collective-permute-done | bytes 524320 | tf_op jit(solution)/shard_map/ppermute | solution.py:12
  155.4 5.8 %all-to-all-start.1 = ((bf16[8,8,128,128]{3,2,1,0:T(8,128)(2,1)}), bf16[8,8,128,128]{3,2,1,0:T(8,128)(2,1)}, u32[]{:S(2)}, u32[]{:S(2)}) async-start(bf16[8,8,128,128]{3,2,1,0:T(8,128)(2,1)} %fusion.16), calls=%async_computation.1 | async-start | bytes 4194304 | tf_op jit(solution)/shard_map/all_to_all | solution.py:54
  161.2 1.5 collective-permute-start.6
  162.6 40.4 %collective-permute-done.6 = f32[8,128]{1,0:T(8,128)S(1)} collective-permute-done((f32[8,128]{1,0:T(8,128)S(1)}, f32[8,128]{1,0:T(8,128)S(1)}, u32[]{:S(2)}, u32[]{:S(2)}) %collective-permute-start.6) | collective-permute-done | bytes 4128 | tf_op jit(solution)/shard_map/ppermute | solution.py:43
  203.0 3.1 %collective-permute-start.7 = (f32[8,128]{1,0:T(8,128)S(1)}, f32[8,128]{1,0:T(8,128)S(1)}, u32[]{:S(2)}, u32[]{:S(2)}) collective-permute-start(f32[8,128]{1,0:T(8,128)S(1)} %collective-permute-done.6), channel_id=1, source_target_pairs={{0,1},{1,2},{2,3},{3,4},{4,5},{5,6},{6,7},{7,0},{8,9},{9,10},{10,1... | collective-permute-start | bytes 12296 | tf_op jit(solution)/shard_map/ppermute | solution.py:43
  206.2 1.3 collective-permute-done.7
  207.5 2.6 %collective-permute-start.8 = (f32[8,128]{1,0:T(8,128)S(1)}, f32[8,128]{1,0:T(8,128)S(1)}, u32[]{:S(2)}, u32[]{:S(2)}) collective-permute-start(f32[8,128]{1,0:T(8,128)S(1)} %collective-permute-done.7), channel_id=1, source_target_pairs={{0,1},{1,2},{2,3},{3,4},{4,5},{5,6},{6,7},{7,0},{8,9},{9,10},{10,1... | collective-permute-start | bytes 12296 | tf_op jit(solution)/shard_map/ppermute | solution.py:43
  210.2 1.3 collective-permute-start.11
  211.5 1.6 collective-permute-done.8
  213.1 1.1 collective-permute-start.9
  214.7 2.0 collective-permute-start.12
  216.6 1.3 collective-permute-done.9
  217.9 1.6 collective-permute-done.12
  219.7 5.2 %fusion.1 = f32[64,128,128]{2,1,0:T(8,128)} fusion(bf16[64,128,128]{2,1,0:T(8,128)(2,1)} %bitcast.21, bf16[128,8192]{1,0:T(8,128)(2,1)S(1)} %copy-done), kind=kOutput, calls=%fused_computation.5 | convolution fusion | flops 268435456 | bytes 8388608 | tf_op jit(solution)/shard_map/bhd,hde->bhe/dot_general | solution.py:56
  224.8 7.6 %multiply_reduce_fusion = (f32[128,64]{0,1:T(8,128)S(1)}, f32[128,64,128]{0,2,1:T(8,128)}) fusion(bf16[128,64,128]{0,2,1:T(8,128)(2,1)} %bitcast.111, bf16[128,64,128]{0,2,1:T(8,128)(2,1)} %bitcast.109, pred[128,128]{1,0:T(8,128)(4,1)S(1)} %iota_compare_fusion, f32[64,128,128]{2,1,0:T(8,128)} %fusion.1, bf16[128,8192]{1,0:T(8,128)(2,1)S(1)} %copy-done), kind=kOutput, calls=%fused_computation.2 | convolution fusion | flops 542105600 | bytes 14729216 | tf_op jit(solution)/shard_map/hbc,chd->bhd/dot_general | solution.py:60
  232.4 3.9 %multiply_convert_fusion = bf16[128,64,128]{0,2,1:T(8,128)(2,1)} fusion(f32[128,64,128]{0,2,1:T(8,128)} %get-tuple-element.10, f32[64,128]{1,0:T(8,128)S(1)} %constant_dynamic-slice_fusion, f32[128,64]{0,1:T(8,128)S(1)} %add_rsqrt_fusion), kind=kLoop, calls=%fused_computation.1 | loop fusion | flops 3145728 | bytes 6356992 | tf_op jit(solution)/shard_map/convert_element_type | solution.py:63
  236.3 4.1 %copy.10 = bf16[128,8192]{1,0:T(8,128)(2,1)} copy(bf16[128,8192]{0,1:T(8,128)(2,1)} %bitcast.112) | data formatting | bytes 4194304 | tf_op jit(solution)/shard_map/reshape | solution.py:64
  (42 shorter events, 8.1 us)
Async XLA Ops:
  0.0 219.7 %copy-start = (bf16[128,8192]{1,0:T(8,128)(2,1)S(1)}, bf16[128,8192]{1,0:T(8,128)(2,1)}, u32[]{:S(2)}) copy-start(bf16[128,8192]{1,0:T(8,128)(2,1)} %param.4) | copy-start | bytes 6291460
  70.5 12.6 %collective-permute-start = (f32[8,128,128]{2,1,0:T(8,128)S(1)}, f32[8,128,128]{2,1,0:T(8,128)S(1)}, u32[]{:S(2)}, u32[]{:S(2)}) collective-permute-start(f32[8,128,128]{2,1,0:T(8,128)S(1)} %convert_reduce_fusion), channel_id=1, source_target_pairs={{0,8},{8,16},{16,24},{24,32},{32,40},{40,48},{48,56},{56,64},{64,7... | collective-permute-start | bytes 1572872 | tf_op jit(solution)/shard_map/ppermute | solution.py:12
  83.2 14.8 %collective-permute-start.1 = (f32[8,128,128]{2,1,0:T(8,128)S(1)}, f32[8,128,128]{2,1,0:T(8,128)S(1)}, u32[]{:S(2)}, u32[]{:S(2)}) collective-permute-start(f32[8,128,128]{2,1,0:T(8,128)S(1)} %add.61), channel_id=1, source_target_pairs={{0,16},{8,24},{16,32},{24,40},{32,48},{40,56},{48,64},{56,72},{64,... | collective-permute-start | bytes 1572872 | tf_op jit(solution)/shard_map/ppermute | solution.py:12
  98.1 14.3 %collective-permute-start.2 = (f32[8,128,128]{2,1,0:T(8,128)S(1)}, f32[8,128,128]{2,1,0:T(8,128)S(1)}, u32[]{:S(2)}, u32[]{:S(2)}) collective-permute-start(f32[8,128,128]{2,1,0:T(8,128)S(1)} %add.62), channel_id=1, source_target_pairs={{0,32},{8,40},{16,48},{24,56},{32,64},{40,72},{48,80},{56,88},{64,... | collective-permute-start | bytes 1572872 | tf_op jit(solution)/shard_map/ppermute | solution.py:12
  112.5 11.2 %collective-permute-start.3 = (f32[8,128,128]{2,1,0:T(8,128)S(1)}, f32[8,128,128]{2,1,0:T(8,128)S(1)}, u32[]{:S(2)}, u32[]{:S(2)}) collective-permute-start(f32[8,128,128]{2,1,0:T(8,128)S(1)} %add.63), channel_id=1, source_target_pairs={{0,64},{8,72},{16,80},{24,88},{32,96},{40,104},{48,112},{56,120},{... | collective-permute-start | bytes 1572872 | tf_op jit(solution)/shard_map/ppermute | solution.py:12
  123.7 12.6 %collective-permute-start.4 = (f32[8,128,128]{2,1,0:T(8,128)S(1)}, f32[8,128,128]{2,1,0:T(8,128)S(1)}, u32[]{:S(2)}, u32[]{:S(2)}) collective-permute-start(f32[8,128,128]{2,1,0:T(8,128)S(1)} %add.64), channel_id=1, source_target_pairs={{0,128},{8,136},{16,144},{24,152},{32,160},{40,168},{48,176},{56,1... | collective-permute-start | bytes 1572872 | tf_op jit(solution)/shard_map/ppermute | solution.py:12
  136.4 12.6 %collective-permute-start.5 = (f32[8,128,128]{2,1,0:T(8,128)S(1)}, f32[8,128,128]{2,1,0:T(8,128)S(1)}, u32[]{:S(2)}, u32[]{:S(2)}) collective-permute-start(f32[8,128,128]{2,1,0:T(8,128)S(1)} %add.65), channel_id=1, source_target_pairs={{0,8},{8,16},{16,24},{24,32},{32,40},{40,48},{48,56},{56,64},{64,7... | collective-permute-start | bytes 1572872 | tf_op jit(solution)/shard_map/ppermute | solution.py:12
  155.4 5.8 %copy-start.1 = (f32[8,128]{1,0:T(8,128)S(1)}, f32[8,128]{1,0:T(8,128)}, u32[]{:S(2)}) copy-start(f32[8,128]{1,0:T(8,128)} %param.7) | copy-start | bytes 12292
  155.4 64.3 %all-to-all-start.1 = ((bf16[8,8,128,128]{3,2,1,0:T(8,128)(2,1)}), bf16[8,8,128,128]{3,2,1,0:T(8,128)(2,1)}, u32[]{:S(2)}, u32[]{:S(2)}) async-start(bf16[8,8,128,128]{3,2,1,0:T(8,128)(2,1)} %fusion.16), calls=%async_computation.1 | async-start | bytes 4194304 | tf_op jit(solution)/shard_map/all_to_all | solution.py:54
  161.2 41.9 %collective-permute-start.6 = (f32[8,128]{1,0:T(8,128)S(1)}, f32[8,128]{1,0:T(8,128)S(1)}, u32[]{:S(2)}, u32[]{:S(2)}) collective-permute-start(f32[8,128]{1,0:T(8,128)S(1)} %copy-done.1), channel_id=1, source_target_pairs={{0,1},{1,2},{2,3},{3,4},{4,5},{5,6},{6,7},{7,0},{8,9},{9,10},{10,1... | collective-permute-start | bytes 12296 | tf_op jit(solution)/shard_map/ppermute | solution.py:43
  203.0 4.5 %collective-permute-start.7 = (f32[8,128]{1,0:T(8,128)S(1)}, f32[8,128]{1,0:T(8,128)S(1)}, u32[]{:S(2)}, u32[]{:S(2)}) collective-permute-start(f32[8,128]{1,0:T(8,128)S(1)} %collective-permute-done.6), channel_id=1, source_target_pairs={{0,1},{1,2},{2,3},{3,4},{4,5},{5,6},{6,7},{7,0},{8,9},{9,10},{10,1... | collective-permute-start | bytes 12296 | tf_op jit(solution)/shard_map/ppermute | solution.py:43
  206.2 4.0 %collective-permute-start.10 = (f32[8,128]{1,0:T(8,128)S(1)}, f32[8,128]{1,0:T(8,128)S(1)}, u32[]{:S(2)}, u32[]{:S(2)}) collective-permute-start(f32[8,128]{1,0:T(8,128)S(1)} %copy-done.1), channel_id=1, source_target_pairs={{0,7},{1,0},{2,1},{3,2},{4,3},{5,4},{6,5},{7,6},{8,15},{9,8},{10,9... | collective-permute-start | bytes 12296 | tf_op jit(solution)/shard_map/ppermute | solution.py:45
  207.5 5.6 %collective-permute-start.8 = (f32[8,128]{1,0:T(8,128)S(1)}, f32[8,128]{1,0:T(8,128)S(1)}, u32[]{:S(2)}, u32[]{:S(2)}) collective-permute-start(f32[8,128]{1,0:T(8,128)S(1)} %collective-permute-done.7), channel_id=1, source_target_pairs={{0,1},{1,2},{2,3},{3,4},{4,5},{5,6},{6,7},{7,0},{8,9},{9,10},{10,1... | collective-permute-start | bytes 12296 | tf_op jit(solution)/shard_map/ppermute | solution.py:43
  210.2 4.5 %collective-permute-start.11 = (f32[8,128]{1,0:T(8,128)S(1)}, f32[8,128]{1,0:T(8,128)S(1)}, u32[]{:S(2)}, u32[]{:S(2)}) collective-permute-start(f32[8,128]{1,0:T(8,128)S(1)} %collective-permute-done.10), channel_id=1, source_target_pairs={{0,7},{1,0},{2,1},{3,2},{4,3},{5,4},{6,5},{7,6},{8,15},{9,8},{10,9... | collective-permute-start | bytes 12296 | tf_op jit(solution)/shard_map/ppermute | solution.py:45
  213.1 4.8 %collective-permute-start.9 = (f32[8,128]{1,0:T(8,128)S(1)}, f32[8,128]{1,0:T(8,128)S(1)}, u32[]{:S(2)}, u32[]{:S(2)}) collective-permute-start(f32[8,128]{1,0:T(8,128)S(1)} %collective-permute-done.8), channel_id=1, source_target_pairs={{0,1},{1,2},{2,3},{3,4},{4,5},{5,6},{6,7},{7,0},{8,9},{9,10},{10,1... | collective-permute-start | bytes 12296 | tf_op jit(solution)/shard_map/ppermute | solution.py:43
  214.7 4.9 %collective-permute-start.12 = (f32[8,128]{1,0:T(8,128)S(1)}, f32[8,128]{1,0:T(8,128)S(1)}, u32[]{:S(2)}, u32[]{:S(2)}) collective-permute-start(f32[8,128]{1,0:T(8,128)S(1)} %collective-permute-done.11), channel_id=1, source_target_pairs={{0,7},{1,0},{2,1},{3,2},{4,3},{5,4},{6,5},{7,6},{8,15},{9,8},{10,9... | collective-permute-start | bytes 12296 | tf_op jit(solution)/shard_map/ppermute | solution.py:45
